TPU v7x, 512 devices: a whole 4x4x16 slice. The times are simulated.
512 devices in a mesh: row: 16 (over z_lo, y), col: 32 (over x, z_hi, core).
Axes of the slice: x: 4, y: 4, z: 16 (z_hi: 4, z_lo: 4; z = z_hi * 4 + z_lo), core: 2. Of those that a mesh axis runs over, the one named last changes fastest.
Arguments:
- tiles: bfloat16 [16, 32, 32, 128, 128], P('row', 'col'), may hold values from -0.5 to 0.5
- tile_slots: int32 [16, 32, 32], P('row', 'col'), may hold values from 0 to 191, as said below
- tile_counts: int32 [16, 32], P('row', 'col'), may hold values from 8 to 32, as said below
- user_degree: int32 [32768], P('row'), may hold values from 1 to 64
- item_degree: int32 [49152], P('col'), may hold values from 1 to 64
- start_panel: float32 [64, 49152], P(None, ('col', 'row')), may hold values from -6 to 6
Outputs:
- left_panel: float32 [64, 32768], P(None, ('row', 'col'))
- right_panel: float32 [64, 49152], P(None, ('col', 'row'))
- left_factors: float32 [3, 64, 64], replicated
- right_factors: float32 [3, 64, 64], replicated
Inputs may be any that keep to these rules, and one draw needn't show every extreme that they name: `tile_slots`: within one grid cell the 32 slot numbers are distinct; slot s is local tile row s // 12 and local tile column s % 12; entries from position tile_counts on are padding. `tile_counts`: some grid cell holds 32 live tiles.
All inputs are finite; a program needn't handle non-finite values.
Results may differ from a plain program's by a relative error of at most 0.0005.
Values sent between devices are 32-bit elements; how exact they have to be, the bound alone decides.
No kernel may reach another device: no remote copies, remote signals or barrier semaphores. Data moves between devices by JAX's collectives and lax.ppermute only.
A program may use at most 64 MiB of HBM per device.

v0:
```python
import math
import jax
import jax.numpy as jnp
from jax import lax
from jax.sharding import PartitionSpec as P

STEPS = 3
HIGH = lax.Precision.HIGHEST


def gram_of(vectors):
    return jnp.einsum("bn,cn->bc", vectors, vectors, precision=HIGH)


def solve_lower(factor, vectors):
    return lax.linalg.triangular_solve(factor, vectors, left_side=True, lower=True)


def per_device(tiles, tile_slots, tile_counts, user_degree, item_degree, start_panel):
    tile_stack = tiles[0, 0].astype(jnp.float32)
    slot_list = tile_slots[0, 0]
    tile_total = tile_counts[0, 0]
    slot_count = tile_stack.shape[0]
    tile_width = tile_stack.shape[1]
    row_blocks = user_degree.shape[0] // tile_width
    col_blocks = item_degree.shape[0] // tile_width
    block_width = start_panel.shape[0]
    live_mask = jnp.arange(slot_count) < tile_total
    local_rows = slot_list // col_blocks
    local_cols = slot_list % col_blocks
    row_select = (
        (local_rows[:, None] == jnp.arange(row_blocks)[None, :]) & live_mask[:, None]
    ).astype(jnp.float32)
    col_select = (
        (local_cols[:, None] == jnp.arange(col_blocks)[None, :]) & live_mask[:, None]
    ).astype(jnp.float32)
    user_scale = lax.rsqrt(user_degree.astype(jnp.float32))
    item_scale = lax.rsqrt(item_degree.astype(jnp.float32))
    user_group = row_blocks * tile_width // lax.axis_size("col")
    item_group = col_blocks * tile_width // lax.axis_size("row")
    user_offset = lax.axis_index("col") * user_group
    item_offset = lax.axis_index("row") * item_group
    user_scale_own = lax.dynamic_slice_in_dim(user_scale, user_offset, user_group)
    item_scale_own = lax.dynamic_slice_in_dim(item_scale, item_offset, item_group)
    start_total = lax.psum(gram_of(start_panel), ("row", "col"))
    start_factor = jnp.linalg.cholesky(start_total)
    item_basis = solve_lower(start_factor, start_panel)
    user_basis = start_panel[:, :0]
    item_factor = start_factor
    user_list = []
    item_list = []
    for iteration in range(STEPS):
        scaled = item_basis * item_scale_own[None, :]
        item_full = lax.all_gather(scaled, "row", axis=1, tiled=True)
        forward_panel_blocks = item_full.reshape(block_width, col_blocks, tile_width)
        forward_chosen = jnp.take(forward_panel_blocks, local_cols, axis=1)
        forward_partial_value = jnp.einsum(
            "mrc,bmc->bmr", tile_stack, forward_chosen, precision=HIGH
        )
        forward_summed = jnp.einsum(
            "bmr,mk->bkr", forward_partial_value, row_select, precision=HIGH
        )
        forward = (
            lax.psum_scatter(
                forward_summed.reshape(block_width, row_blocks * tile_width),
                "col",
                scatter_dimension=1,
                tiled=True,
            )
            * user_scale_own[None, :]
        )
        if iteration > 0:
            forward = forward - jnp.dot(item_factor.T, user_basis, precision=HIGH)
        user_factor = jnp.linalg.cholesky(lax.psum(gram_of(forward), ("row", "col")))
        user_basis = solve_lower(user_factor, forward)
        scaled = user_basis * user_scale_own[None, :]
        user_full = lax.all_gather(scaled, "col", axis=1, tiled=True)
        panel_blocks = user_full.reshape(block_width, row_blocks, tile_width)
        chosen = jnp.take(panel_blocks, local_rows, axis=1)
        partial_value = jnp.einsum("mrc,bmr->bmc", tile_stack, chosen, precision=HIGH)
        summed = jnp.einsum("bmc,mk->bkc", partial_value, col_select, precision=HIGH)
        backward = (
            lax.psum_scatter(
                summed.reshape(block_width, col_blocks * tile_width),
                "row",
                scatter_dimension=1,
                tiled=True,
            )
            * item_scale_own[None, :]
        )
        backward = backward - jnp.dot(user_factor.T, item_basis, precision=HIGH)
        item_factor = jnp.linalg.cholesky(lax.psum(gram_of(backward), ("row", "col")))
        item_basis = solve_lower(item_factor, backward)
        user_list.append(user_factor)
        item_list.append(item_factor)
    user_total = row_blocks * tile_width * lax.axis_size("row")
    item_total = col_blocks * tile_width * lax.axis_size("col")
    return (
        math.sqrt(user_total) * user_basis,
        math.sqrt(item_total) * item_basis,
        jnp.stack(user_list),
        jnp.stack(item_list),
    )


def solution(mesh):
    in_specs = (
        P("row", "col", None, None, None),
        P("row", "col", None),
        P("row", "col"),
        P("row"),
        P("col"),
        P(None, ("col", "row")),
    )
    out_specs = (P(None, ("row", "col")), P(None, ("col", "row")), P(), P())
    return jax.shard_map(
        per_device, mesh=mesh, in_specs=in_specs, out_specs=out_specs, check_vma=False
    )
```

profile of v0, /device:TPU:1, one launch (start us, length us, event | category | flops | bytes accessed | tf_op | source)
XLA Modules:
  0.0 1727.9 jit_solution(9248479124465914468)
XLA Ops:
  8.7 1.0 fusion.153
  9.7 111.2 %psum.49 = f32[64,64]{0,1:T(8,128)S(1)} all-reduce(f32[64,64]{0,1:T(8,128)S(1)} %fusion.153), channel_id=1, replica_groups=mesh['row'=16,'col'=32] {'row','col'}, use_global_device_ids=true, to_apply=%region_0.1 | all-reduce | flops 4096 | bytes 32768 | tf_op jit(solution)/shard_map/psum | solution.py:45
  120.9 5.8 cholesky.119
  128.1 4.9 custom-call.13
  134.1 33.8 %all-gather = f32[16,96,64]{1,2,0:T(8,128)S(1)} all-gather(f32[1,96,64]{1,2,0:T(8,128)S(1)} %multiply_bitcast_fusion.2), channel_id=1, replica_groups=mesh['row'=16,'col'=32] {'row'}, dimensions={0}, use_global_device_ids=true | all-gather | bytes 417792 | tf_op jit(solution)/shard_map/all_gather | solution.py:54
  169.1 2.2 convolution_bitcast_fusion.5
  171.3 1.1 convolution_bitcast_fusion.11
  172.4 1.4 copy.162
  174.6 110.4 %reduce-scatter.19.cloned.1.call-done = f32[64,64]{1,0:T(8,128)} async-done(((f32[2048,64]{1,0:T(8,128)}), f32[64,64]{1,0:T(8,128)}) %reduce-scatter.19.cloned.1.call-update) | async-done | bytes 16400
  285.0 0.8 copy.151
  286.0 101.8 %psum.50 = f32[64,64]{0,1:T(8,128)S(1)} all-reduce(f32[64,64]{0,1:T(8,128)S(1)} %fusion.81), channel_id=1, replica_groups=mesh['row'=16,'col'=32] {'row','col'}, use_global_device_ids=true, to_apply=%region_4.8 | all-reduce | flops 4096 | bytes 32768 | tf_op jit(solution)/shard_map/psum | solution.py:74
  388.0 5.8 cholesky.130
  395.1 4.9 custom-call.14
  400.4 57.0 %all_gather.19 = f32[64,2048]{0,1:T(8,128)S(1)} all-gather(f32[64,64]{0,1:T(8,128)S(1)} %copy.109), channel_id=1, replica_groups=mesh['row'=16,'col'=32] {'col'}, dimensions={1}, use_global_device_ids=true | all-gather | bytes 540672 | tf_op jit(solution)/shard_map/all_gather | solution.py:77
  458.3 1.0 convolution_bitcast_fusion.4
  459.3 1.1 convolution_bitcast_fusion.10
  460.4 1.2 copy.163
  461.6 71.2 %reduce-scatter.21.cloned.1.call-done = f32[96,64]{1,0:T(8,128)} async-done(((f32[1536,64]{1,0:T(8,128)}), f32[96,64]{1,0:T(8,128)}) %reduce-scatter.21.cloned.1.call-update) | async-done | bytes 24592
  532.8 0.9 copy.153
  533.7 0.9 convolution_subtract_fusion.4
  534.8 112.8 %psum.51 = f32[64,64]{0,1:T(8,128)S(1)} all-reduce(f32[64,64]{0,1:T(8,128)S(1)} %fusion.154), channel_id=1, replica_groups=mesh['row'=16,'col'=32] {'row','col'}, use_global_device_ids=true, to_apply=%region_6.12 | all-reduce | flops 4096 | bytes 32768 | tf_op jit(solution)/shard_map/psum | solution.py:92
  647.7 5.8 cholesky.141
  654.9 4.9 custom-call.15
  660.0 36.4 %all-gather.1 = f32[16,96,64]{1,2,0:T(8,128)S(1)} all-gather(f32[1,96,64]{1,2,0:T(8,128)S(1)} %multiply_bitcast_fusion.1), channel_id=1, replica_groups=mesh['row'=16,'col'=32] {'row'}, dimensions={0}, use_global_device_ids=true | all-gather | bytes 417792 | tf_op jit(solution)/shard_map/all_gather | solution.py:54
  697.6 2.2 convolution_bitcast_fusion.3
  699.8 1.1 convolution_bitcast_fusion.9
  700.9 1.4 copy.164
  702.3 110.1 %reduce-scatter.23.cloned.1.call-done = f32[64,64]{1,0:T(8,128)} async-done(((f32[2048,64]{1,0:T(8,128)}), f32[64,64]{1,0:T(8,128)}) %reduce-scatter.23.cloned.1.call-update) | async-done | bytes 16400
  812.4 0.8 copy.155
  813.2 0.9 convolution_subtract_fusion.3
  814.3 102.0 %psum.52 = f32[64,64]{0,1:T(8,128)S(1)} all-reduce(f32[64,64]{0,1:T(8,128)S(1)} %fusion.155), channel_id=1, replica_groups=mesh['row'=16,'col'=32] {'row','col'}, use_global_device_ids=true, to_apply=%region_8.14 | all-reduce | flops 4096 | bytes 32768 | tf_op jit(solution)/shard_map/psum | solution.py:74
  916.4 5.8 cholesky.152
  923.6 4.9 custom-call.16
  928.9 56.4 %all_gather.21 = f32[64,2048]{0,1:T(8,128)S(1)} all-gather(f32[64,64]{0,1:T(8,128)S(1)} %copy.120), channel_id=1, replica_groups=mesh['row'=16,'col'=32] {'col'}, dimensions={1}, use_global_device_ids=true | all-gather | bytes 540672 | tf_op jit(solution)/shard_map/all_gather | solution.py:77
  986.2 1.0 convolution_bitcast_fusion.2
  987.2 1.1 convolution_bitcast_fusion.8
  988.3 1.2 copy.165
  989.6 70.9 %reduce-scatter.25.cloned.1.call-done = f32[96,64]{1,0:T(8,128)} async-done(((f32[1536,64]{1,0:T(8,128)}), f32[96,64]{1,0:T(8,128)}) %reduce-scatter.25.cloned.1.call-update) | async-done | bytes 24592
  1060.5 0.9 copy.157
  1061.4 0.9 convolution_subtract_fusion.2
  1062.5 113.1 %psum.53 = f32[64,64]{0,1:T(8,128)S(1)} all-reduce(f32[64,64]{0,1:T(8,128)S(1)} %fusion.156), channel_id=1, replica_groups=mesh['row'=16,'col'=32] {'row','col'}, use_global_device_ids=true, to_apply=%region_10.16 | all-reduce | flops 4096 | bytes 32768 | tf_op jit(solution)/shard_map/psum | solution.py:92
  1175.6 5.8 cholesky.163
  1182.8 4.9 custom-call.17
  1188.0 36.7 %all-gather.2 = f32[16,96,64]{1,2,0:T(8,128)S(1)} all-gather(f32[1,96,64]{1,2,0:T(8,128)S(1)} %multiply_bitcast_fusion), channel_id=1, replica_groups=mesh['row'=16,'col'=32] {'row'}, dimensions={0}, use_global_device_ids=true | all-gather | bytes 417792 | tf_op jit(solution)/shard_map/all_gather | solution.py:54
  1225.9 2.2 convolution_bitcast_fusion.1
  1228.0 1.1 convolution_bitcast_fusion.7
  1229.1 1.4 copy.166
  1230.5 110.1 %reduce-scatter.27.cloned.1.call-done = f32[64,64]{1,0:T(8,128)} async-done(((f32[2048,64]{1,0:T(8,128)}), f32[64,64]{1,0:T(8,128)}) %reduce-scatter.27.cloned.1.call-update) | async-done | bytes 16400
  1341.4 0.9 convolution_subtract_fusion.1
  1342.5 101.8 %psum.54 = f32[64,64]{0,1:T(8,128)S(1)} all-reduce(f32[64,64]{0,1:T(8,128)S(1)} %fusion.157), channel_id=1, replica_groups=mesh['row'=16,'col'=32] {'row','col'}, use_global_device_ids=true, to_apply=%region_12.18 | all-reduce | flops 4096 | bytes 32768 | tf_op jit(solution)/shard_map/psum | solution.py:74
  1444.4 5.8 cholesky.174
  1451.6 4.9 custom-call.18
  1456.5 0.9 broadcast_multiply_fusion.1
  1457.5 56.3 %all_gather.23 = f32[64,2048]{0,1:T(8,128)S(1)} all-gather(f32[64,64]{0,1:T(8,128)S(1)} %copy.131), channel_id=1, replica_groups=mesh['row'=16,'col'=32] {'col'}, dimensions={1}, use_global_device_ids=true | all-gather | bytes 540672 | tf_op jit(solution)/shard_map/all_gather | solution.py:77
  1514.7 1.0 convolution_bitcast_fusion
  1515.7 1.1 convolution_bitcast_fusion.6
  1516.8 1.2 copy.167
  1518.7 73.4 %reduce-scatter.29.cloned.1.call-done = f32[96,64]{1,0:T(8,128)} async-done(((f32[1536,64]{1,0:T(8,128)}), f32[96,64]{1,0:T(8,128)}) %reduce-scatter.29.cloned.1.call-update) | async-done | bytes 24592
  1592.0 0.9 copy.161
  1592.9 0.9 convolution_subtract_fusion
  1594.0 113.0 %psum.55 = f32[64,64]{0,1:T(8,128)S(1)} all-reduce(f32[64,64]{0,1:T(8,128)S(1)} %fusion.158), channel_id=1, replica_groups=mesh['row'=16,'col'=32] {'row','col'}, use_global_device_ids=true, to_apply=%region_14.20 | all-reduce | flops 4096 | bytes 32768 | tf_op jit(solution)/shard_map/psum | solution.py:92
  1707.1 5.8 cholesky.185
  1714.3 4.9 custom-call.19
  1719.2 0.9 convolution_multiply_fusion
  (98 shorter events, 23.6 us)
Async XLA Ops:
  7.2 161.9 %copy-start = (bf16[1,1,32,128,128]{4,3,2,1,0:T(8,128)(2,1)S(1)}, bf16[1,1,32,128,128]{4,3,2,1,0:T(8,128)(2,1)}, u32[]{:S(2)}) copy-start(bf16[1,1,32,128,128]{4,3,2,1,0:T(8,128)(2,1)} %param.15) | copy-start | bytes 3145732
  7.2 277.8 %reduce-scatter.19.cloned.1.call-start = ((), (), s32[]{:S(2)}) async-start(), calls=%async_computation.6 | async-start | bytes 1081344
  8.0 0.7 copy-start.2
  127.5 5.6 copy-start.1
  173.7 359.1 %reduce-scatter.21.cloned.1.call-start = ((), (), s32[]{:S(2)}) async-start(), calls=%async_computation.7 | async-start | bytes 835584
  461.6 350.8 %reduce-scatter.23.cloned.1.call-start = ((), (), s32[]{:S(2)}) async-start(), calls=%async_computation.8 | async-start | bytes 1081344
  702.3 358.2 %reduce-scatter.25.cloned.1.call-start = ((), (), s32[]{:S(2)}) async-start(), calls=%async_computation.9 | async-start | bytes 835584
  989.5 351.1 %reduce-scatter.27.cloned.1.call-start = ((), (), s32[]{:S(2)}) async-start(), calls=%async_computation.10 | async-start | bytes 1081344
  1230.5 361.6 %reduce-scatter.29.cloned.1.call-start = ((), (), s32[]{:S(2)}) async-start(), calls=%async_computation.11 | async-start | bytes 835584
Sparse Core Ops, SparseCore 0:
  173.9 111.0 reduce-scatter.18
  461.7 71.0 reduce-scatter.20
  702.4 109.9 reduce-scatter.22
  989.6 70.8 reduce-scatter.24
  1230.6 109.9 reduce-scatter.26
  1518.1 73.8 reduce-scatter.28
where the time goes:
time: 1740 us; the launch traced here: 1730 us
  blocking collectives  1030 us (59%)
  waiting for transfers between devices  546 us (31%)
  other arithmetic  87.5 us (5%)
  matrix products  25.6 us (1%)
  local copies, waits for them, and re-layouts  20.4 us (1%)
    unnamed x12, waiting for transfers between devices  546 us
    psum x3, blocking collectives, per_device(): lax.psum(gram_of(backward), ('row', 'col'))  339 us
    psum x3, blocking collectives, per_device(): lax.psum(gram_of(forward), ('row', 'col'))  306 us
    all_gather x3, blocking collectives, per_device(): user_full = lax.all_gather(scaled, 'col', axis=1, tiled=True)  170 us
    psum x1, blocking collectives, per_device(): start_total = lax.psum(gram_of(start_panel), ('row', 'col'))  111 us
    all_gather x3, blocking collectives, per_device(): item_full = lax.all_gather(scaled, 'row', axis=1, tiled=True)  107 us
    another operation x8, other arithmetic, solve_lower(): lax.linalg.triangular_solve(factor, vectors, left_side=True, lower=True)  34.9 us
  transfers between devices with their start and end apart: 6, of which 6 were waited for; matrix products, arithmetic and copies ran while one was open for 0% of the time, Pallas kernels for 0%

commit v1 on v0

--- a/solution.py
+++ b/solution.py
@@ -89,7 +89,9 @@
             * item_scale_own[None, :]
         )
         backward = backward - jnp.dot(user_factor.T, item_basis, precision=HIGH)
-        item_factor = jnp.linalg.cholesky(lax.psum(gram_of(backward), ("row", "col")))
+        item_factor = jnp.linalg.cholesky(
+            jnp.sum(lax.all_gather(gram_of(backward), ("row", "col")), axis=0)
+        )
         item_basis = solve_lower(item_factor, backward)
         user_list.append(user_factor)
         item_list.append(item_factor)

time: 1740 us -> 3950 us (2.27)
  waiting for transfers between devices: 546 us -> 3070 us
  blocking collectives: 1030 us -> 688 us
    all_gather x0 -> x3, waiting for transfers between devices: none -> 2520 us  [per_device(): lax.all_gather(gram_of(backward), ('row', 'col'))]
    psum x3 -> x0, blocking collectives: 339 us -> none  [per_device(): lax.psum(gram_of(backward), ('row', 'col'))]
    unnamed x12 -> x15, waiting for transfers between devices: 546 us -> 559 us
  transfers between devices with their start and end apart: 6 -> 9, of which waited for: 6 -> 9; matrix products, arithmetic and copies ran while one was open for 0% -> 0% of each run, Pallas kernels for 0% -> 0%
where the time goes in v1:
time: 3950 us; the launch traced here: 3930 us
  waiting for transfers between devices  3070 us (78%)
  blocking collectives  688 us (17%)
  other arithmetic  109 us (3%)
    all_gather x3, waiting for transfers between devices, per_device(): lax.all_gather(gram_of(backward), ('row', 'col'))  2520 us
    unnamed x15, waiting for transfers between devices  559 us
    psum x3, blocking collectives, per_device(): lax.psum(gram_of(forward), ('row', 'col'))  306 us
    all_gather x3, blocking collectives, per_device(): user_full = lax.all_gather(scaled, 'col', axis=1, tiled=True)  170 us
    psum x1, blocking collectives, per_device(): start_total = lax.psum(gram_of(start_panel), ('row', 'col'))  111 us
    all_gather x3, blocking collectives, per_device(): item_full = lax.all_gather(scaled, 'row', axis=1, tiled=True)  101 us
  transfers between devices with their start and end apart: 9, of which 9 were waited for; matrix products, arithmetic and copies ran while one was open for 0% of the time, Pallas kernels for 0%

profile of v1, /device:TPU:1, one launch (start us, length us, event | category | flops | bytes accessed | tf_op | source)
XLA Modules:
  0.0 3934.4 jit_solution(6143887757101990867)
XLA Ops:
  8.7 1.0 fusion.153
  9.7 111.2 %psum.28 = f32[64,64]{0,1:T(8,128)S(1)} all-reduce(f32[64,64]{0,1:T(8,128)S(1)} %fusion.153), channel_id=1, replica_groups=mesh['row'=16,'col'=32] {'row','col'}, use_global_device_ids=true, to_apply=%region_0.1 | all-reduce | flops 4096 | bytes 32768 | tf_op jit(solution)/shard_map/psum | solution.py:45
  120.9 5.8 cholesky.119
  128.1 4.9 custom-call.13
  133.0 1.0 fusion.54
  134.8 33.8 all-gather.3
  169.8 2.2 convolution_bitcast_fusion.5
  172.0 1.1 convolution_bitcast_fusion.11
  173.1 1.4 copy.144
  175.3 110.4 %reduce-scatter.19.cloned.1.call-done = f32[64,64]{1,0:T(8,128)} async-done(((f32[2048,64]{1,0:T(8,128)}), f32[64,64]{1,0:T(8,128)}) %reduce-scatter.19.cloned.1.call-update) | async-done | bytes 16400
  286.7 101.9 %psum.29 = f32[64,64]{0,1:T(8,128)S(1)} all-reduce(f32[64,64]{0,1:T(8,128)S(1)} %fusion.81), channel_id=1, replica_groups=mesh['row'=16,'col'=32] {'row','col'}, use_global_device_ids=true, to_apply=%region_4.8 | all-reduce | flops 4096 | bytes 32768 | tf_op jit(solution)/shard_map/psum | solution.py:74
  388.7 5.8 cholesky.130
  395.9 4.9 custom-call.14
  401.1 56.9 %all_gather.37 = f32[64,2048]{0,1:T(8,128)S(1)} all-gather(f32[64,64]{0,1:T(8,128)S(1)} %copy.97), channel_id=1, replica_groups=mesh['row'=16,'col'=32] {'col'}, dimensions={1}, use_global_device_ids=true | all-gather | bytes 540672 | tf_op jit(solution)/shard_map/all_gather | solution.py:77
  459.0 1.0 convolution_bitcast_fusion.4
  460.0 1.1 convolution_bitcast_fusion.10
  461.1 1.2 copy.145
  462.4 70.5 %reduce-scatter.21.cloned.1.call-done = f32[96,64]{1,0:T(8,128)} async-done(((f32[1536,64]{1,0:T(8,128)}), f32[96,64]{1,0:T(8,128)}) %reduce-scatter.21.cloned.1.call-update) | async-done | bytes 24592
  532.9 0.9 copy.135
  533.7 0.9 convolution_subtract_fusion.4
  535.5 838.4 %all-gather.10.cloned.1.call-done = f32[32768,64]{1,0:T(8,128)} async-done(((f32[64,64]{1,0:T(8,128)}), f32[32768,64]{1,0:T(8,128)}) %all-gather.10.cloned.1.call-update) | async-done | bytes 8388624 | tf_op jit(solution)/shard_map/all_gather | solution.py:93
  1373.9 6.9 reduce_sum.27
  1381.0 5.8 cholesky.141
  1388.2 4.9 custom-call.15
  1393.3 33.5 all-gather.4
  1428.0 2.2 convolution_bitcast_fusion.3
  1430.2 1.1 convolution_bitcast_fusion.9
  1431.3 1.4 copy.146
  1432.7 118.3 %reduce-scatter.23.cloned.1.call-done = f32[64,64]{1,0:T(8,128)} async-done(((f32[2048,64]{1,0:T(8,128)}), f32[64,64]{1,0:T(8,128)}) %reduce-scatter.23.cloned.1.call-update) | async-done | bytes 16400
  1551.8 0.9 convolution_subtract_fusion.3
  1552.9 102.0 %psum.30 = f32[64,64]{0,1:T(8,128)S(1)} all-reduce(f32[64,64]{0,1:T(8,128)S(1)} %fusion.155), channel_id=1, replica_groups=mesh['row'=16,'col'=32] {'row','col'}, use_global_device_ids=true, to_apply=%region_8.14 | all-reduce | flops 4096 | bytes 32768 | tf_op jit(solution)/shard_map/psum | solution.py:74
  1655.0 5.8 cholesky.152
  1662.2 4.9 custom-call.16
  1667.4 56.7 %all_gather.41 = f32[64,2048]{0,1:T(8,128)S(1)} all-gather(f32[64,64]{0,1:T(8,128)S(1)} %copy.107), channel_id=1, replica_groups=mesh['row'=16,'col'=32] {'col'}, dimensions={1}, use_global_device_ids=true | all-gather | bytes 540672 | tf_op jit(solution)/shard_map/all_gather | solution.py:77
  1725.1 1.0 convolution_bitcast_fusion.2
  1726.1 1.1 convolution_bitcast_fusion.8
  1727.2 1.2 copy.147
  1728.4 70.5 %reduce-scatter.25.cloned.1.call-done = f32[96,64]{1,0:T(8,128)} async-done(((f32[1536,64]{1,0:T(8,128)}), f32[96,64]{1,0:T(8,128)}) %reduce-scatter.25.cloned.1.call-update) | async-done | bytes 24592
  1799.8 0.9 convolution_subtract_fusion.2
  1801.6 838.6 %all-gather.12.cloned.1.call-done = f32[32768,64]{1,0:T(8,128)} async-done(((f32[64,64]{1,0:T(8,128)}), f32[32768,64]{1,0:T(8,128)}) %all-gather.12.cloned.1.call-update) | async-done | bytes 8388624 | tf_op jit(solution)/shard_map/all_gather | solution.py:93
  2640.2 6.9 reduce_sum.28
  2647.3 5.8 cholesky.163
  2654.5 4.9 custom-call.17
  2659.6 33.7 all-gather.5
  2694.5 2.2 convolution_bitcast_fusion.1
  2696.7 1.1 convolution_bitcast_fusion.7
  2697.8 1.4 copy.148
  2699.2 118.3 %reduce-scatter.27.cloned.1.call-done = f32[64,64]{1,0:T(8,128)} async-done(((f32[2048,64]{1,0:T(8,128)}), f32[64,64]{1,0:T(8,128)}) %reduce-scatter.27.cloned.1.call-update) | async-done | bytes 16400
  2818.3 0.9 convolution_subtract_fusion.1
  2819.4 101.8 %psum.31 = f32[64,64]{0,1:T(8,128)S(1)} all-reduce(f32[64,64]{0,1:T(8,128)S(1)} %fusion.157), channel_id=1, replica_groups=mesh['row'=16,'col'=32] {'row','col'}, use_global_device_ids=true, to_apply=%region_12.18 | all-reduce | flops 4096 | bytes 32768 | tf_op jit(solution)/shard_map/psum | solution.py:74
  2921.3 5.8 cholesky.174
  2928.5 4.9 custom-call.18
  2933.4 0.9 broadcast_multiply_fusion.1
  2934.4 56.4 %all_gather.45 = f32[64,2048]{0,1:T(8,128)S(1)} all-gather(f32[64,64]{0,1:T(8,128)S(1)} %copy.117), channel_id=1, replica_groups=mesh['row'=16,'col'=32] {'col'}, dimensions={1}, use_global_device_ids=true | all-gather | bytes 540672 | tf_op jit(solution)/shard_map/all_gather | solution.py:77
  2991.7 1.0 convolution_bitcast_fusion
  2992.7 1.1 convolution_bitcast_fusion.6
  2993.8 1.2 copy.149
  2995.3 70.4 %reduce-scatter.29.cloned.1.call-done = f32[96,64]{1,0:T(8,128)} async-done(((f32[1536,64]{1,0:T(8,128)}), f32[96,64]{1,0:T(8,128)}) %reduce-scatter.29.cloned.1.call-update) | async-done | bytes 24592
  3066.6 0.9 convolution_subtract_fusion
  3069.0 838.0 %all-gather.14.cloned.1.call-done = f32[32768,64]{1,0:T(8,128)} async-done(((f32[64,64]{1,0:T(8,128)}), f32[32768,64]{1,0:T(8,128)}) %all-gather.14.cloned.1.call-update) | async-done | bytes 8388624 | tf_op jit(solution)/shard_map/all_gather | solution.py:93
  3906.9 6.9 reduce_sum.29
  3914.0 5.8 cholesky.185
  3921.2 4.9 custom-call.19
  3926.0 0.9 convolution_multiply_fusion
  (103 shorter events, 29.0 us)
Async XLA Ops:
  7.2 162.7 %copy-start = (bf16[1,1,32,128,128]{4,3,2,1,0:T(8,128)(2,1)S(1)}, bf16[1,1,32,128,128]{4,3,2,1,0:T(8,128)(2,1)}, u32[]{:S(2)}) copy-start(bf16[1,1,32,128,128]{4,3,2,1,0:T(8,128)(2,1)} %param.15) | copy-start | bytes 3145732
  7.2 278.5 %reduce-scatter.19.cloned.1.call-start = ((), (), s32[]{:S(2)}) async-start(), calls=%async_computation.9 | async-start | bytes 1081344
  174.5 358.4 %reduce-scatter.21.cloned.1.call-start = ((), (), s32[]{:S(2)}) async-start(), calls=%async_computation.10 | async-start | bytes 835584
  462.3 911.6 %all-gather.10.cloned.1.call-start = ((), (), s32[]{:S(2)}) async-start(), calls=%async_computation.6 | async-start | bytes 16809984 | tf_op jit(solution)/shard_map/all_gather | solution.py:93
  535.5 1015.5 %reduce-scatter.23.cloned.1.call-start = ((), (), s32[]{:S(2)}) async-start(), calls=%async_computation.11 | async-start | bytes 1081344
  1432.6 366.3 %reduce-scatter.25.cloned.1.call-start = ((), (), s32[]{:S(2)}) async-start(), calls=%async_computation.12 | async-start | bytes 835584
  1728.4 911.9 %all-gather.12.cloned.1.call-start = ((), (), s32[]{:S(2)}) async-start(), calls=%async_computation.7 | async-start | bytes 16809984 | tf_op jit(solution)/shard_map/all_gather | solution.py:93
  1801.6 1015.9 %reduce-scatter.27.cloned.1.call-start = ((), (), s32[]{:S(2)}) async-start(), calls=%async_computation.13 | async-start | bytes 1081344
  2699.1 366.6 %reduce-scatter.29.cloned.1.call-start = ((), (), s32[]{:S(2)}) async-start(), calls=%async_computation.14 | async-start | bytes 835584
  2995.0 912.0 %all-gather.14.cloned.1.call-start = ((), (), s32[]{:S(2)}) async-start(), calls=%async_computation.8 | async-start | bytes 16809984 | tf_op jit(solution)/shard_map/all_gather | solution.py:93
Sparse Core Ops, SparseCore 0:
  174.6 111.0 reduce-scatter.18
  462.4 70.3 reduce-scatter.20
  535.7 838.2 all-gather.9
  1432.8 118.1 reduce-scatter.22
  1728.5 70.4 reduce-scatter.24
  1801.7 838.4 all-gather.11
  2699.3 118.1 reduce-scatter.26
  2995.1 70.5 reduce-scatter.28
  3068.5 838.3 all-gather.13
